TPU v7x, 512 devices: a whole 4x8x8 slice. The times are simulated.
512 devices in a mesh: group: 8 (over y), mesh: 32 (over z, x), comp: 2 (over core).
Axes of the slice: x: 4, y: 8, z: 8, core: 2. Of those that a mesh axis runs over, the one named last changes fastest.
Arguments:
- log_sigma: float32 [2048, 128], P('mesh'), may hold values from -1 to 1
- block_owner: int32 [8, 4096, 1], P('group', 'mesh'), may hold values from 0 to 31; in each aligned block of 128 rows (0 to 127, 128 to 255, ..., all dimensions but the last counted through in order) at most 8 rows name the same one
- block_slot: int32 [8, 4096], P('group', 'mesh'), may hold values from 0 to 63
- coupling: float32 [128, 128], replicated, may hold values from -0.6 to 10, as said below
- sources: float32 [8, 2, 8, 4096, 128], P('group', 'comp', None, 'mesh'), may hold values from -24 to 24
- rcv_cell: int32 [8, 4096], P('group', 'mesh'), may hold values from 0 to 16383
- observed: float32 [8, 2, 8, 4096], P('group', 'comp', None, 'mesh'), may hold values from -6 to 6
Outputs:
- gradient: float32 [2048, 128], P('mesh')
Inputs may be any that keep to these rules, and one draw needn't show every extreme that they name: `block_owner`: in the 128 rows of one device of a group, no owner is named more than 8 times; some owner is named exactly 8 times in some device's rows. `rcv_cell`: A receiver's cell counts from the first cell of the modelling section of the device that holds the receiver's entry. `coupling`: every diagonal entry is 6 or more.
All inputs are finite; a program needn't handle non-finite values.
Results may differ from a plain program's by a relative error of at most 0.0003.
Values sent between devices are 32-bit elements; how exact they have to be, the bound alone decides.
A program may use at most 64 MiB of HBM per device.

v0:
```python
import jax
import jax.numpy as jnp
from jax import lax
from jax.sharding import PartitionSpec as P

CELLS = 128
S = 8
ITERS = 6
omega_freq = 0.8
chain_weight = 1.0


def from_partner(value, axis, distance):
    mask = 2**distance
    pairs = [(source, source ^ mask) for source in range(lax.axis_size(axis))]
    return lax.ppermute(value, axis, pairs)


def with_halo(x, sides, width):
    for axis, dim in sides:
        size, length = (lax.axis_size(axis), x.shape[dim])
        up = [(i, (i + 1) % size) for i in range(size - 1)]
        down = [(j, i) for i, j in up]
        last = lax.slice_in_dim(x, length - width, length, axis=dim)
        initial = lax.slice_in_dim(x, 0, width, axis=dim)
        before = lax.ppermute(last, axis, up)
        after = lax.ppermute(initial, axis, down)
        x = jnp.concatenate([before, x, after], axis=dim)
    return x


def partner(values):
    return from_partner(values, "comp", 0)


def beside(values):
    padded = with_halo(values, (("mesh", 1),), 1)
    return padded[:, :-2] + padded[:, 2:]


def cell_product(values, matrix):
    shaped = values.reshape(values.shape[:-1] + (-1, CELLS))
    product = jnp.einsum("...bj,ij->...bi", shaped, matrix, precision=lax.Precision.HIGHEST)
    return product.reshape(values.shape)


def operate(values, matrix, cross_coef):
    return (
        cell_product(values, matrix) - chain_weight * beside(values) + cross_coef * partner(values)
    )


def relax(right, matrix, cross_coef, inverse_diag, apply_op):
    state = jnp.zeros_like(right)
    for iteration in range(ITERS):
        state = state + inverse_diag * (right - apply_op(state, matrix, cross_coef))
    return state


def local(log_sigma, block_owner, block_slot, coupling, sources, rcv_cell, observed):
    owners = block_owner[0, :, 0]
    slots = block_slot[0]
    blocks_dev = owners.shape[0]
    inv_rows = log_sigma.shape[0]
    targets = owners * inv_rows + slots
    gathered = lax.all_gather(log_sigma, "mesh", axis=0, tiled=True)
    model_part = jnp.take(gathered, targets, axis=0)
    sigmas = jnp.exp(model_part).reshape(-1)
    receivers = rcv_cell[0]
    parity = (2 * lax.axis_index("comp") - 1).astype(jnp.float32)
    forward_coef = parity * omega_freq * sigmas
    inverse_diag = jnp.tile(1.0 / jnp.diagonal(coupling), blocks_dev)
    right = sources.reshape(S, -1)
    field_now = relax(right, coupling, forward_coef, inverse_diag, operate)
    field_other = partner(field_now)
    misfit = field_now[:, receivers] - observed[0, 0]
    adjoint_src = jnp.zeros_like(right).at[:, receivers].add(misfit)
    adjoint = relax(adjoint_src, coupling.T, -forward_coef, inverse_diag, operate)
    weighted = -parity * jnp.sum(adjoint * field_other, axis=0)
    partial_rows = (omega_freq * sigmas * weighted).reshape(blocks_dev, CELLS)
    inside_rows = (targets >= 0) & (targets < inv_rows * lax.axis_size("mesh"))
    kept_rows = jnp.where(inside_rows, targets, inv_rows * lax.axis_size("mesh"))
    owned = lax.psum_scatter(
        jnp.zeros((inv_rows * lax.axis_size("mesh"), CELLS), jnp.float32)
        .at[kept_rows]
        .add(partial_rows, mode="drop"),
        "mesh",
        scatter_dimension=0,
        tiled=True,
    )
    return lax.psum(owned, ("group", "comp"))


def solution(mesh):
    in_specs = (
        P("mesh", None),
        P("group", "mesh", None),
        P("group", "mesh"),
        P(),
        P("group", "comp", None, "mesh", None),
        P("group", "mesh"),
        P("group", "comp", None, "mesh"),
    )
    out_specs = P("mesh", None)
    return jax.shard_map(local, mesh=mesh, in_specs=in_specs, out_specs=out_specs, check_vma=False)
```

profile of v0, /device:TPU:32, one launch (start us, length us, event | category | flops | bytes accessed | tf_op | source)
XLA Modules:
  0.0 532.8 jit_solution(2460921501740615536)
XLA Ops:
  6.5 0.7 all-gather.2.cloned.1.call-update
  7.3 1.3 collective-permute-start.1
  8.6 4.5 collective-permute-start
  13.2 1.9 collective-permute-start.2
  15.2 1.2 gather_fusion.1
  17.0 0.7 compare_and_fusion
  17.7 0.7 fusion.121
  18.4 78.7 %all-gather.2.cloned.1.call-done = f32[2048,128]{1,0:T(8,128)} async-done(((f32[64,128]{1,0:T(8,128)}), f32[2048,128]{1,0:T(8,128)}) %all-gather.2.cloned.1.call-update) | async-done | bytes 1048592 | tf_op jit(solution)/shard_map/all_gather | solution.py:66
  97.1 1.9 gather_fusion
  99.1 1.7 fusion.8
  100.8 1.9 collective-permute-start.5
  102.8 1.3 collective-permute-start.4
  104.1 4.5 collective-permute-start.3
  108.6 1.3 collective-permute-done.3
  109.9 1.9 fusion.10
  111.9 1.9 collective-permute-start.8
  113.9 1.3 collective-permute-start.7
  115.2 4.8 collective-permute-start.6
  120.0 0.6 convolution_bitcast_fusion.8
  120.6 0.7 collective-permute-done.6
  121.8 1.9 collective-permute-start.11
  123.8 1.3 collective-permute-start.10
  125.1 4.8 collective-permute-start.9
  129.9 1.3 collective-permute-done.9
  131.2 0.9 fusion.14
  132.1 1.9 collective-permute-start.14
  134.1 1.3 collective-permute-start.13
  135.4 4.8 collective-permute-start.12
  140.2 0.6 convolution_bitcast_fusion.6
  140.8 0.7 collective-permute-done.12
  142.1 1.9 collective-permute-start.17
  144.8 1.3 collective-permute-start.16
  146.1 5.5 %collective-permute-start.15 = (f32[8,1]{1,0:T(8,128)S(1)}, f32[8,1]{1,0:T(8,128)S(1)}, u32[]{:S(2)}, u32[]{:S(2)}) collective-permute-start(f32[8,1]{1,0:T(8,128)S(1)} %get-tuple-element.17), channel_id=1, source_target_pairs={{0,2},{2,4},{4,6},{6,8},{8,10},{10,12},{12,14},{14,16},{16,18},{18... | collective-permute-start | bytes 104 | tf_op jit(solution)/shard_map/ppermute | solution.py:26
  151.6 1.3 collective-permute-done.15
  152.9 1.9 fusion.18
  154.8 5.3 copy.271
  160.1 6.0 %scatter_custom_fusion = f32[8,16384]{0,1:T(8,128)} fusion(s32[128]{0:T(128)S(1)} %fusion.122, f32[]{:T(128)} %constant.12.clone.1, f32[1,1,8,128]{2,3,1,0:T(8,128)S(1)} %copy.272, f32[8,16384]{0,1:T(8,128)} %copy.271, s32[1024]{0:T(1024)S(1)} %pad_clamp_fusion), kind=kCustom, calls=%fused_computation.15 | custom fusion | flops 2048 | bytes 1118212 | tf_op jit(solution)/shard_map/scatter-add | solution.py:77
  166.1 5.5 %copy.273 = f32[8,16384]{1,0:T(8,128)S(1)} copy(f32[8,16384]{0,1:T(8,128)} %scatter_custom_fusion) | data formatting | bytes 1048576 | tf_op jit(solution)/shard_map/scatter-add | solution.py:77
  172.0 1.9 collective-permute-start.20
  174.0 1.3 collective-permute-start.19
  175.3 6.9 %collective-permute-start.18 = (f32[8,1]{1,0:T(8,128)S(1)}, f32[8,1]{1,0:T(8,128)S(1)}, u32[]{:S(2)}, u32[]{:S(2)}) collective-permute-start(f32[8,1]{1,0:T(8,128)S(1)} %get-tuple-element.15), channel_id=1, source_target_pairs={{0,2},{2,4},{4,6},{6,8},{8,10},{10,12},{12,14},{14,16},{16,18},{18... | collective-permute-start | bytes 104 | tf_op jit(solution)/shard_map/ppermute | solution.py:26
  182.3 1.3 collective-permute-done.18
  183.6 0.7 fusion.50
  184.2 1.9 collective-permute-start.23
  186.2 1.3 collective-permute-start.22
  187.5 6.9 %collective-permute-start.21 = (f32[8,1]{1,0:T(8,128)S(1)}, f32[8,1]{1,0:T(8,128)S(1)}, u32[]{:S(2)}, u32[]{:S(2)}) collective-permute-start(f32[8,1]{1,0:T(8,128)S(1)} %get-tuple-element.13), channel_id=1, source_target_pairs={{0,2},{2,4},{4,6},{6,8},{8,10},{10,12},{12,14},{14,16},{16,18},{18... | collective-permute-start | bytes 104 | tf_op jit(solution)/shard_map/ppermute | solution.py:26
  195.0 0.7 collective-permute-done.21
  196.2 1.9 collective-permute-start.26
  198.2 1.3 collective-permute-start.25
  199.5 6.9 %collective-permute-start.24 = (f32[8,1]{1,0:T(8,128)S(1)}, f32[8,1]{1,0:T(8,128)S(1)}, u32[]{:S(2)}, u32[]{:S(2)}) collective-permute-start(f32[8,1]{1,0:T(8,128)S(1)} %get-tuple-element.11), channel_id=1, source_target_pairs={{0,2},{2,4},{4,6},{6,8},{8,10},{10,12},{12,14},{14,16},{16,18},{18... | collective-permute-start | bytes 104 | tf_op jit(solution)/shard_map/ppermute | solution.py:26
  206.4 1.3 collective-permute-done.24
  207.7 0.7 fusion.38
  208.4 1.9 collective-permute-start.29
  210.3 2.4 collective-permute-start.33
  212.8 1.3 collective-permute-start.28
  214.1 6.9 %collective-permute-start.27 = (f32[8,1]{1,0:T(8,128)S(1)}, f32[8,1]{1,0:T(8,128)S(1)}, u32[]{:S(2)}, u32[]{:S(2)}) collective-permute-start(f32[8,1]{1,0:T(8,128)S(1)} %get-tuple-element.9), channel_id=1, source_target_pairs={{0,2},{2,4},{4,6},{6,8},{8,10},{10,12},{12,14},{14,16},{16,18},{18... | collective-permute-start | bytes 104 | tf_op jit(solution)/shard_map/ppermute | solution.py:26
  221.6 0.7 collective-permute-done.27
  222.8 1.9 collective-permute-start.32
  224.8 1.3 collective-permute-start.31
  226.1 6.9 %collective-permute-start.30 = (f32[8,1]{1,0:T(8,128)S(1)}, f32[8,1]{1,0:T(8,128)S(1)}, u32[]{:S(2)}, u32[]{:S(2)}) collective-permute-start(f32[8,1]{1,0:T(8,128)S(1)} %get-tuple-element.7), channel_id=1, source_target_pairs={{0,2},{2,4},{4,6},{6,8},{8,10},{10,12},{12,14},{14,16},{16,18},{18... | collective-permute-start | bytes 104 | tf_op jit(solution)/shard_map/ppermute | solution.py:26
  233.6 0.7 collective-permute-done.30
  234.7 2.1 scatter_custom_fusion.1
  236.8 242.3 %reduce-scatter.2.cloned.1.call-done = f32[64,128]{1,0:T(8,128)} async-done(((f32[2048,128]{1,0:T(8,128)}), f32[64,128]{1,0:T(8,128)}) %reduce-scatter.2.cloned.1.call-update) | async-done | bytes 32784 | tf_op jit(solution)/shard_map/reduce_scatter | solution.py:83
  479.1 46.9 %psum.7 = f32[64,128]{1,0:T(8,128)} all-reduce(f32[64,128]{1,0:T(8,128)} %reduce-scatter.2.cloned.1.call-done), channel_id=1, replica_groups=mesh['group'=8,'mesh'=32,'comp'=2] {'group','comp'}, use_global_device_ids=true, to_apply=%region_4.5 | all-reduce | flops 8192 | bytes 65536 | tf_op jit(solution)/shard_map/psum | solution.py:91
  (66 shorter events, 6.6 us)
Async XLA Ops:
  6.5 8.7 %copy-start = (f32[128,128]{1,0:T(8,128)S(1)}, f32[128,128]{1,0:T(8,128)}, u32[]{:S(2)}) copy-start(f32[128,128]{1,0:T(8,128)} %param.10) | copy-start | bytes 196612
  6.5 114.8 %copy-start.1 = (f32[1,1,8,128,128]{4,3,2,1,0:T(8,128)S(1)}, f32[1,1,8,128,128]{4,3,2,1,0:T(8,128)}, u32[]{:S(2)}) copy-start(f32[1,1,8,128,128]{4,3,2,1,0:T(8,128)} %param.11) | copy-start | bytes 1572868
  6.5 90.6 %all-gather.2.cloned.1.call-start = ((), (), s32[]{:S(2)}) async-start(), calls=%async_computation.1 | async-start | bytes 1081344 | tf_op jit(solution)/shard_map/all_gather | solution.py:66
  7.3 471.8 %reduce-scatter.2.cloned.1.call-start = ((), (), s32[]{:S(2)}) async-start(), calls=%async_computation.2 | async-start | bytes 1081344 | tf_op jit(solution)/shard_map/reduce_scatter | solution.py:83
  7.3 91.8 %collective-permute-start.1 = (f32[8,1]{1,0:T(8,128)S(1)}, f32[8,1]{1,0:T(8,128)S(1)}, u32[]{:S(2)}, u32[]{:S(2)}) collective-permute-start(f32[8,1]{1,0:T(8,128)S(1)} %broadcast.157), channel_id=1, source_target_pairs={{2,0},{4,2},{6,4},{8,6},{10,8},{12,10},{14,12},{16,14},{18,16},{20... | collective-permute-start | bytes 104 | tf_op jit(solution)/shard_map/ppermute | solution.py:27
  8.6 90.5 %collective-permute-start = (f32[8,1]{1,0:T(8,128)S(1)}, f32[8,1]{1,0:T(8,128)S(1)}, u32[]{:S(2)}, u32[]{:S(2)}) collective-permute-start(f32[8,1]{1,0:T(8,128)S(1)} %broadcast.157), channel_id=1, source_target_pairs={{0,2},{2,4},{4,6},{6,8},{8,10},{10,12},{12,14},{14,16},{16,18},{18... | collective-permute-start | bytes 104 | tf_op jit(solution)/shard_map/ppermute | solution.py:26
  13.2 130.8 %copy-start.3 = (s32[1,128]{1,0:T(1,128)S(1)}, s32[1,128]{1,0:T(1,128)}, u32[]{:S(2)}) copy-start(s32[1,128]{1,0:T(1,128)} %param.12) | copy-start | bytes 1540
  13.2 130.8 %copy-start.2 = (f32[1,1,8,128]{3,2,1,0:T(8,128)S(1)}, f32[1,1,8,128]{3,2,1,0:T(8,128)}, u32[]{:S(2)}) copy-start(f32[1,1,8,128]{3,2,1,0:T(8,128)} %param.13) | copy-start | bytes 12292
  13.2 85.8 %collective-permute-start.2 = (f32[8,16384]{1,0:T(8,128)S(1)}, f32[8,16384]{1,0:T(8,128)S(1)}, u32[]{:S(2)}, u32[]{:S(2)}) collective-permute-start(f32[8,16384]{1,0:T(8,128)S(1)} %broadcast.154.clone), channel_id=1, source_target_pairs={{0,1},{1,0},{2,3},{3,2},{4,5},{5,4},{6,7},{7,6},{8,9},{9,8},{10,11... | collective-permute-start | bytes 1572872 | tf_op jit(solution)/shard_map/ppermute | solution.py:16
  100.8 9.2 %collective-permute-start.5 = (f32[8,16384]{1,0:T(8,128)S(1)}, f32[8,16384]{1,0:T(8,128)S(1)}, u32[]{:S(2)}, u32[]{:S(2)}) collective-permute-start(f32[8,16384]{1,0:T(8,128)S(1)} %fusion.8), channel_id=1, source_target_pairs={{0,1},{1,0},{2,3},{3,2},{4,5},{5,4},{6,7},{7,6},{8,9},{9,8},{10,11... | collective-permute-start | bytes 1572872 | tf_op jit(solution)/shard_map/ppermute | solution.py:16
  102.8 5.8 %collective-permute-start.4 = (f32[8,1]{1,0:T(8,128)S(1)}, f32[8,1]{1,0:T(8,128)S(1)}, u32[]{:S(2)}, u32[]{:S(2)}) collective-permute-start(f32[8,1]{1,0:T(8,128)S(1)} %get-tuple-element.26), channel_id=1, source_target_pairs={{2,0},{4,2},{6,4},{8,6},{10,8},{12,10},{14,12},{16,14},{18,16},{20... | collective-permute-start | bytes 104 | tf_op jit(solution)/shard_map/ppermute | solution.py:27
  104.1 5.9 %collective-permute-start.3 = (f32[8,1]{1,0:T(8,128)S(1)}, f32[8,1]{1,0:T(8,128)S(1)}, u32[]{:S(2)}, u32[]{:S(2)}) collective-permute-start(f32[8,1]{1,0:T(8,128)S(1)} %get-tuple-element.25), channel_id=1, source_target_pairs={{0,2},{2,4},{4,6},{6,8},{8,10},{10,12},{12,14},{14,16},{16,18},{18... | collective-permute-start | bytes 104 | tf_op jit(solution)/shard_map/ppermute | solution.py:26
  111.9 9.4 %collective-permute-start.8 = (f32[8,16384]{1,0:T(8,128)S(1)}, f32[8,16384]{1,0:T(8,128)S(1)}, u32[]{:S(2)}, u32[]{:S(2)}) collective-permute-start(f32[8,16384]{1,0:T(8,128)S(1)} %fusion.10), channel_id=1, source_target_pairs={{0,1},{1,0},{2,3},{3,2},{4,5},{5,4},{6,7},{7,6},{8,9},{9,8},{10,11... | collective-permute-start | bytes 1572872 | tf_op jit(solution)/shard_map/ppermute | solution.py:16
  113.9 6.7 %collective-permute-start.7 = (f32[8,1]{1,0:T(8,128)S(1)}, f32[8,1]{1,0:T(8,128)S(1)}, u32[]{:S(2)}, u32[]{:S(2)}) collective-permute-start(f32[8,1]{1,0:T(8,128)S(1)} %get-tuple-element.24), channel_id=1, source_target_pairs={{2,0},{4,2},{6,4},{8,6},{10,8},{12,10},{14,12},{16,14},{18,16},{20... | collective-permute-start | bytes 104 | tf_op jit(solution)/shard_map/ppermute | solution.py:27
  115.2 6.1 %collective-permute-start.6 = (f32[8,1]{1,0:T(8,128)S(1)}, f32[8,1]{1,0:T(8,128)S(1)}, u32[]{:S(2)}, u32[]{:S(2)}) collective-permute-start(f32[8,1]{1,0:T(8,128)S(1)} %get-tuple-element.23), channel_id=1, source_target_pairs={{0,2},{2,4},{4,6},{6,8},{8,10},{10,12},{12,14},{14,16},{16,18},{18... | collective-permute-start | bytes 104 | tf_op jit(solution)/shard_map/ppermute | solution.py:26
  121.8 9.4 %collective-permute-start.11 = (f32[8,16384]{1,0:T(8,128)S(1)}, f32[8,16384]{1,0:T(8,128)S(1)}, u32[]{:S(2)}, u32[]{:S(2)}) collective-permute-start(f32[8,16384]{1,0:T(8,128)S(1)} %fusion.12), channel_id=1, source_target_pairs={{0,1},{1,0},{2,3},{3,2},{4,5},{5,4},{6,7},{7,6},{8,9},{9,8},{10,11... | collective-permute-start | bytes 1572872 | tf_op jit(solution)/shard_map/ppermute | solution.py:16
  123.8 6.1 %collective-permute-start.10 = (f32[8,1]{1,0:T(8,128)S(1)}, f32[8,1]{1,0:T(8,128)S(1)}, u32[]{:S(2)}, u32[]{:S(2)}) collective-permute-start(f32[8,1]{1,0:T(8,128)S(1)} %get-tuple-element.22), channel_id=1, source_target_pairs={{2,0},{4,2},{6,4},{8,6},{10,8},{12,10},{14,12},{16,14},{18,16},{20... | collective-permute-start | bytes 104 | tf_op jit(solution)/shard_map/ppermute | solution.py:27
  125.1 6.1 %collective-permute-start.9 = (f32[8,1]{1,0:T(8,128)S(1)}, f32[8,1]{1,0:T(8,128)S(1)}, u32[]{:S(2)}, u32[]{:S(2)}) collective-permute-start(f32[8,1]{1,0:T(8,128)S(1)} %get-tuple-element.21), channel_id=1, source_target_pairs={{0,2},{2,4},{4,6},{6,8},{8,10},{10,12},{12,14},{14,16},{16,18},{18... | collective-permute-start | bytes 104 | tf_op jit(solution)/shard_map/ppermute | solution.py:26
  132.1 9.4 %collective-permute-start.14 = (f32[8,16384]{1,0:T(8,128)S(1)}, f32[8,16384]{1,0:T(8,128)S(1)}, u32[]{:S(2)}, u32[]{:S(2)}) collective-permute-start(f32[8,16384]{1,0:T(8,128)S(1)} %fusion.14), channel_id=1, source_target_pairs={{0,1},{1,0},{2,3},{3,2},{4,5},{5,4},{6,7},{7,6},{8,9},{9,8},{10,11... | collective-permute-start | bytes 1572872 | tf_op jit(solution)/shard_map/ppermute | solution.py:16
  134.1 6.7 %collective-permute-start.13 = (f32[8,1]{1,0:T(8,128)S(1)}, f32[8,1]{1,0:T(8,128)S(1)}, u32[]{:S(2)}, u32[]{:S(2)}) collective-permute-start(f32[8,1]{1,0:T(8,128)S(1)} %get-tuple-element.20), channel_id=1, source_target_pairs={{2,0},{4,2},{6,4},{8,6},{10,8},{12,10},{14,12},{16,14},{18,16},{20... | collective-permute-start | bytes 104 | tf_op jit(solution)/shard_map/ppermute | solution.py:27
  135.4 6.1 %collective-permute-start.12 = (f32[8,1]{1,0:T(8,128)S(1)}, f32[8,1]{1,0:T(8,128)S(1)}, u32[]{:S(2)}, u32[]{:S(2)}) collective-permute-start(f32[8,1]{1,0:T(8,128)S(1)} %get-tuple-element.19), channel_id=1, source_target_pairs={{0,2},{2,4},{4,6},{6,8},{8,10},{10,12},{12,14},{14,16},{16,18},{18... | collective-permute-start | bytes 104 | tf_op jit(solution)/shard_map/ppermute | solution.py:26
  142.1 10.8 %collective-permute-start.17 = (f32[8,16384]{1,0:T(8,128)S(1)}, f32[8,16384]{1,0:T(8,128)}, u32[]{:S(2)}, u32[]{:S(2)}) collective-permute-start(f32[8,16384]{1,0:T(8,128)S(1)} %fusion.16), channel_id=1, source_target_pairs={{0,1},{1,0},{2,3},{3,2},{4,5},{5,4},{6,7},{7,6},{8,9},{9,8},{10,11... | collective-permute-start | bytes 1572872 | tf_op jit(solution)/shard_map/ppermute | solution.py:16
  144.8 6.8 %collective-permute-start.16 = (f32[8,1]{1,0:T(8,128)S(1)}, f32[8,1]{1,0:T(8,128)S(1)}, u32[]{:S(2)}, u32[]{:S(2)}) collective-permute-start(f32[8,1]{1,0:T(8,128)S(1)} %get-tuple-element.18), channel_id=1, source_target_pairs={{2,0},{4,2},{6,4},{8,6},{10,8},{12,10},{14,12},{16,14},{18,16},{20... | collective-permute-start | bytes 104 | tf_op jit(solution)/shard_map/ppermute | solution.py:27
  146.1 6.8 %collective-permute-start.15 = (f32[8,1]{1,0:T(8,128)S(1)}, f32[8,1]{1,0:T(8,128)S(1)}, u32[]{:S(2)}, u32[]{:S(2)}) collective-permute-start(f32[8,1]{1,0:T(8,128)S(1)} %get-tuple-element.17), channel_id=1, source_target_pairs={{0,2},{2,4},{4,6},{6,8},{8,10},{10,12},{12,14},{14,16},{16,18},{18... | collective-permute-start | bytes 104 | tf_op jit(solution)/shard_map/ppermute | solution.py:26
  172.0 11.5 %collective-permute-start.20 = (f32[8,16384]{1,0:T(8,128)S(1)}, f32[8,16384]{1,0:T(8,128)S(1)}, u32[]{:S(2)}, u32[]{:S(2)}) collective-permute-start(f32[8,16384]{1,0:T(8,128)S(1)} %fusion.5), channel_id=1, source_target_pairs={{0,1},{1,0},{2,3},{3,2},{4,5},{5,4},{6,7},{7,6},{8,9},{9,8},{10,11... | collective-permute-start | bytes 1572872 | tf_op jit(solution)/shard_map/ppermute | solution.py:16
  174.0 8.2 %collective-permute-start.19 = (f32[8,1]{1,0:T(8,128)S(1)}, f32[8,1]{1,0:T(8,128)S(1)}, u32[]{:S(2)}, u32[]{:S(2)}) collective-permute-start(f32[8,1]{1,0:T(8,128)S(1)} %get-tuple-element.16), channel_id=1, source_target_pairs={{2,0},{4,2},{6,4},{8,6},{10,8},{12,10},{14,12},{16,14},{18,16},{20... | collective-permute-start | bytes 104 | tf_op jit(solution)/shard_map/ppermute | solution.py:27
  175.3 8.3 %collective-permute-start.18 = (f32[8,1]{1,0:T(8,128)S(1)}, f32[8,1]{1,0:T(8,128)S(1)}, u32[]{:S(2)}, u32[]{:S(2)}) collective-permute-start(f32[8,1]{1,0:T(8,128)S(1)} %get-tuple-element.15), channel_id=1, source_target_pairs={{0,2},{2,4},{4,6},{6,8},{8,10},{10,12},{12,14},{14,16},{16,18},{18... | collective-permute-start | bytes 104 | tf_op jit(solution)/shard_map/ppermute | solution.py:26
  184.2 11.5 %collective-permute-start.23 = (f32[8,16384]{1,0:T(8,128)S(1)}, f32[8,16384]{1,0:T(8,128)S(1)}, u32[]{:S(2)}, u32[]{:S(2)}) collective-permute-start(f32[8,16384]{1,0:T(8,128)S(1)} %fusion.50), channel_id=1, source_target_pairs={{0,1},{1,0},{2,3},{3,2},{4,5},{5,4},{6,7},{7,6},{8,9},{9,8},{10,11... | collective-permute-start | bytes 1572872 | tf_op jit(solution)/shard_map/ppermute | solution.py:16
  186.2 8.8 %collective-permute-start.22 = (f32[8,1]{1,0:T(8,128)S(1)}, f32[8,1]{1,0:T(8,128)S(1)}, u32[]{:S(2)}, u32[]{:S(2)}) collective-permute-start(f32[8,1]{1,0:T(8,128)S(1)} %get-tuple-element.14), channel_id=1, source_target_pairs={{2,0},{4,2},{6,4},{8,6},{10,8},{12,10},{14,12},{16,14},{18,16},{20... | collective-permute-start | bytes 104 | tf_op jit(solution)/shard_map/ppermute | solution.py:27
  187.5 8.2 %collective-permute-start.21 = (f32[8,1]{1,0:T(8,128)S(1)}, f32[8,1]{1,0:T(8,128)S(1)}, u32[]{:S(2)}, u32[]{:S(2)}) collective-permute-start(f32[8,1]{1,0:T(8,128)S(1)} %get-tuple-element.13), channel_id=1, source_target_pairs={{0,2},{2,4},{4,6},{6,8},{8,10},{10,12},{12,14},{14,16},{16,18},{18... | collective-permute-start | bytes 104 | tf_op jit(solution)/shard_map/ppermute | solution.py:26
  196.2 11.5 %collective-permute-start.26 = (f32[8,16384]{1,0:T(8,128)S(1)}, f32[8,16384]{1,0:T(8,128)S(1)}, u32[]{:S(2)}, u32[]{:S(2)}) collective-permute-start(f32[8,16384]{1,0:T(8,128)S(1)} %fusion.44), channel_id=1, source_target_pairs={{0,1},{1,0},{2,3},{3,2},{4,5},{5,4},{6,7},{7,6},{8,9},{9,8},{10,11... | collective-permute-start | bytes 1572872 | tf_op jit(solution)/shard_map/ppermute | solution.py:16
  198.2 8.2 %collective-permute-start.25 = (f32[8,1]{1,0:T(8,128)S(1)}, f32[8,1]{1,0:T(8,128)S(1)}, u32[]{:S(2)}, u32[]{:S(2)}) collective-permute-start(f32[8,1]{1,0:T(8,128)S(1)} %get-tuple-element.12), channel_id=1, source_target_pairs={{2,0},{4,2},{6,4},{8,6},{10,8},{12,10},{14,12},{16,14},{18,16},{20... | collective-permute-start | bytes 104 | tf_op jit(solution)/shard_map/ppermute | solution.py:27
  199.5 8.2 %collective-permute-start.24 = (f32[8,1]{1,0:T(8,128)S(1)}, f32[8,1]{1,0:T(8,128)S(1)}, u32[]{:S(2)}, u32[]{:S(2)}) collective-permute-start(f32[8,1]{1,0:T(8,128)S(1)} %get-tuple-element.11), channel_id=1, source_target_pairs={{0,2},{2,4},{4,6},{6,8},{8,10},{10,12},{12,14},{14,16},{16,18},{18... | collective-permute-start | bytes 104 | tf_op jit(solution)/shard_map/ppermute | solution.py:26
  208.4 14.0 %collective-permute-start.29 = (f32[8,16384]{1,0:T(8,128)S(1)}, f32[8,16384]{1,0:T(8,128)S(1)}, u32[]{:S(2)}, u32[]{:S(2)}) collective-permute-start(f32[8,16384]{1,0:T(8,128)S(1)} %fusion.38), channel_id=1, source_target_pairs={{0,1},{1,0},{2,3},{3,2},{4,5},{5,4},{6,7},{7,6},{8,9},{9,8},{10,11... | collective-permute-start | bytes 1572872 | tf_op jit(solution)/shard_map/ppermute | solution.py:16
  210.3 23.2 %collective-permute-start.33 = (f32[8,16384]{1,0:T(8,128)S(1)}, f32[8,16384]{1,0:T(8,128)S(1)}, u32[]{:S(2)}, u32[]{:S(2)}) collective-permute-start(f32[8,16384]{1,0:T(8,128)S(1)} %fusion.18), channel_id=1, source_target_pairs={{0,1},{1,0},{2,3},{3,2},{4,5},{5,4},{6,7},{7,6},{8,9},{9,8},{10,11... | collective-permute-start | bytes 1572872 | tf_op jit(solution)/shard_map/ppermute | solution.py:16
  212.8 8.8 %collective-permute-start.28 = (f32[8,1]{1,0:T(8,128)S(1)}, f32[8,1]{1,0:T(8,128)S(1)}, u32[]{:S(2)}, u32[]{:S(2)}) collective-permute-start(f32[8,1]{1,0:T(8,128)S(1)} %get-tuple-element.10), channel_id=1, source_target_pairs={{2,0},{4,2},{6,4},{8,6},{10,8},{12,10},{14,12},{16,14},{18,16},{20... | collective-permute-start | bytes 104 | tf_op jit(solution)/shard_map/ppermute | solution.py:27
  214.1 8.3 %collective-permute-start.27 = (f32[8,1]{1,0:T(8,128)S(1)}, f32[8,1]{1,0:T(8,128)S(1)}, u32[]{:S(2)}, u32[]{:S(2)}) collective-permute-start(f32[8,1]{1,0:T(8,128)S(1)} %get-tuple-element.9), channel_id=1, source_target_pairs={{0,2},{2,4},{4,6},{6,8},{8,10},{10,12},{12,14},{14,16},{16,18},{18... | collective-permute-start | bytes 104 | tf_op jit(solution)/shard_map/ppermute | solution.py:26
  222.8 11.5 %collective-permute-start.32 = (f32[8,16384]{1,0:T(8,128)S(1)}, f32[8,16384]{1,0:T(8,128)S(1)}, u32[]{:S(2)}, u32[]{:S(2)}) collective-permute-start(f32[8,16384]{1,0:T(8,128)S(1)} %fusion.32), channel_id=1, source_target_pairs={{0,1},{1,0},{2,3},{3,2},{4,5},{5,4},{6,7},{7,6},{8,9},{9,8},{10,11... | collective-permute-start | bytes 1572872 | tf_op jit(solution)/shard_map/ppermute | solution.py:16
  224.8 8.8 %collective-permute-start.31 = (f32[8,1]{1,0:T(8,128)S(1)}, f32[8,1]{1,0:T(8,128)S(1)}, u32[]{:S(2)}, u32[]{:S(2)}) collective-permute-start(f32[8,1]{1,0:T(8,128)S(1)} %get-tuple-element.8), channel_id=1, source_target_pairs={{2,0},{4,2},{6,4},{8,6},{10,8},{12,10},{14,12},{16,14},{18,16},{20... | collective-permute-start | bytes 104 | tf_op jit(solution)/shard_map/ppermute | solution.py:27
  226.1 8.2 %collective-permute-start.30 = (f32[8,1]{1,0:T(8,128)S(1)}, f32[8,1]{1,0:T(8,128)S(1)}, u32[]{:S(2)}, u32[]{:S(2)}) collective-permute-start(f32[8,1]{1,0:T(8,128)S(1)} %get-tuple-element.7), channel_id=1, source_target_pairs={{0,2},{2,4},{4,6},{6,8},{8,10},{10,12},{12,14},{14,16},{16,18},{18... | collective-permute-start | bytes 104 | tf_op jit(solution)/shard_map/ppermute | solution.py:26
Sparse Core Ops, SparseCore 0:
  10.5 86.5 all-gather.1
  237.0 242.0 reduce-scatter.1
where the time goes:
time: 534 us; the launch traced here: 533 us
  waiting for transfers between devices  332 us (62%)
  starting transfers between devices  101 us (19%)
  blocking collectives  46.9 us (9%)
  local copies, waits for them, and re-layouts  14.9 us (3%)
  between operations  14 us (3%)
  other arithmetic  13.9 us (3%)
  matrix products  10.1 us (2%)
    reduce_scatter x1, waiting for transfers between devices, local(): lax.psum_scatter(jnp.zeros((inv_rows * lax.axis_size('mesh'), CELLS), jnp...  242 us
    all_gather x1, waiting for transfers between devices, local(): gathered = lax.all_gather(log_sigma, 'mesh', axis=0, tiled=True)  78.7 us
    ppermute x11, starting transfers between devices, with_halo(): before = lax.ppermute(last, axis, up)  63.6 us
    psum x1, blocking collectives, local(): return lax.psum(owned, ('group', 'comp'))  46.9 us
    ppermute x12, starting transfers between devices, from_partner(): return lax.ppermute(value, axis, pairs)  23.5 us
    ppermute x11, starting transfers between devices, with_halo(): after = lax.ppermute(initial, axis, down)  14.1 us
  transfers between devices with their start and end apart: 36, of which 12 were waited for; matrix products, arithmetic and copies ran while one was open for 2% of the time, Pallas kernels for 0%

commit v1 on v0

--- a/solution.py
+++ b/solution.py
@@ -8,6 +8,11 @@
 ITERS = 6
 omega_freq = 0.8
 chain_weight = 1.0
+
+
+def summed_here(x, name):
+    parts = lax.all_gather(x, name)
+    return jnp.sum(parts, axis=0)
 
 
 def from_partner(value, axis, distance):
@@ -88,7 +93,7 @@
         scatter_dimension=0,
         tiled=True,
     )
-    return lax.psum(owned, ("group", "comp"))
+    return summed_here(owned, ("group", "comp"))
 
 
 def solution(mesh):

time: 534 us -> 508 us (0.951)
  the two profiles are of different devices: /device:TPU:32 before, /device:TPU:1 now
where the time goes in v1:
time: 508 us; the launch traced here: 507 us
  waiting for transfers between devices  311 us (61%)
  starting transfers between devices  118 us (23%)
  blocking collectives  24.3 us (5%)
  local copies, waits for them, and re-layouts  14.9 us (3%)
  other arithmetic  14.5 us (3%)
  between operations  14 us (3%)
  matrix products  10.1 us (2%)
    reduce_scatter x1, waiting for transfers between devices, local(): lax.psum_scatter(jnp.zeros((inv_rows * lax.axis_size('mesh'), CELLS), jnp...  237 us
    all_gather x1, waiting for transfers between devices, local(): gathered = lax.all_gather(log_sigma, 'mesh', axis=0, tiled=True)  68.6 us
    ppermute x11, starting transfers between devices, with_halo(): before = lax.ppermute(last, axis, up)  60.6 us
    ppermute x12, starting transfers between devices, from_partner(): return lax.ppermute(value, axis, pairs)  43.4 us
    all_gather x1, blocking collectives, summed_here(): parts = lax.all_gather(x, name)  24.3 us
    ppermute x11, starting transfers between devices, with_halo(): after = lax.ppermute(initial, axis, down)  14.1 us
  transfers between devices with their start and end apart: 36, of which 12 were waited for; matrix products, arithmetic and copies ran while one was open for 2% of the time, Pallas kernels for 0%

profile of v1, /device:TPU:1, one launch (start us, length us, event | category | flops | bytes accessed | tf_op | source)
XLA Modules:
  0.0 507.0 jit_solution(10799320339603767849)
XLA Ops:
  6.5 0.7 all-gather.3.cloned.1.call-update
  7.3 1.3 collective-permute-start.1
  8.6 4.6 collective-permute-start
  13.3 8.8 %collective-permute-start.2 = (f32[8,16384]{1,0:T(8,128)S(1)}, f32[8,16384]{1,0:T(8,128)S(1)}, u32[]{:S(2)}, u32[]{:S(2)}) collective-permute-start(f32[8,16384]{1,0:T(8,128)S(1)} %broadcast.154.clone), channel_id=1, source_target_pairs={{0,1},{1,0},{2,3},{3,2},{4,5},{5,4},{6,7},{7,6},{8,9},{9,8},{10,11... | collective-permute-start | bytes 1572872 | tf_op jit(solution)/shard_map/ppermute | solution.py:21
  22.1 1.2 gather_fusion.1
  23.3 0.6 convolution_bitcast_fusion.11
  23.9 0.7 compare_and_fusion
  24.6 0.7 fusion.121
  25.3 68.6 %all-gather.3.cloned.1.call-done = f32[2048,128]{1,0:T(8,128)} async-done(((f32[64,128]{1,0:T(8,128)}), f32[2048,128]{1,0:T(8,128)}) %all-gather.3.cloned.1.call-update) | async-done | bytes 1048592 | tf_op jit(solution)/shard_map/all_gather | solution.py:71
  93.9 1.9 gather_fusion
  95.9 1.7 fusion.8
  97.5 7.0 %collective-permute-start.5 = (f32[8,16384]{1,0:T(8,128)S(1)}, f32[8,16384]{1,0:T(8,128)S(1)}, u32[]{:S(2)}, u32[]{:S(2)}) collective-permute-start(f32[8,16384]{1,0:T(8,128)S(1)} %fusion.8), channel_id=1, source_target_pairs={{0,1},{1,0},{2,3},{3,2},{4,5},{5,4},{6,7},{7,6},{8,9},{9,8},{10,11... | collective-permute-start | bytes 1572872 | tf_op jit(solution)/shard_map/ppermute | solution.py:21
  104.6 1.3 collective-permute-start.4
  105.9 4.0 collective-permute-start.3
  109.9 0.7 collective-permute-done.3
  110.7 1.9 fusion.10
  112.6 3.1 collective-permute-start.8
  115.7 1.3 collective-permute-start.7
  117.0 4.5 collective-permute-start.6
  121.6 0.6 convolution_bitcast_fusion.8
  122.8 2.8 collective-permute-start.11
  125.7 1.3 collective-permute-start.10
  126.9 4.5 collective-permute-start.9
  131.5 0.7 collective-permute-done.9
  132.2 0.9 fusion.14
  133.1 2.8 collective-permute-start.14
  136.0 1.3 collective-permute-start.13
  137.3 4.5 collective-permute-start.12
  141.8 0.6 convolution_bitcast_fusion.6
  143.1 2.8 collective-permute-start.17
  146.6 1.3 collective-permute-start.16
  147.9 5.2 %collective-permute-start.15 = (f32[8,1]{1,0:T(8,128)S(1)}, f32[8,1]{1,0:T(8,128)S(1)}, u32[]{:S(2)}, u32[]{:S(2)}) collective-permute-start(f32[8,1]{1,0:T(8,128)S(1)} %get-tuple-element.17), channel_id=1, source_target_pairs={{0,2},{2,4},{4,6},{6,8},{8,10},{10,12},{12,14},{14,16},{16,18},{18... | collective-permute-start | bytes 104 | tf_op jit(solution)/shard_map/ppermute | solution.py:31
  153.1 0.7 collective-permute-done.15
  153.9 1.9 fusion.18
  155.8 5.3 %copy.383 = f32[8,16384]{0,1:T(8,128)} copy(f32[8,16384]{1,0:T(8,128)S(1)} %fusion.18) | data formatting | bytes 1048576 | tf_op jit(solution)/shard_map/add | solution.py:61
  161.1 6.0 %scatter_custom_fusion = f32[8,16384]{0,1:T(8,128)} fusion(s32[128]{0:T(128)S(1)} %fusion.122, f32[]{:T(128)} %constant.12.clone.1, f32[1,1,8,128]{2,3,1,0:T(8,128)S(1)} %copy.384, f32[8,16384]{0,1:T(8,128)} %copy.383, s32[1024]{0:T(1024)S(1)} %pad_clamp_fusion), kind=kCustom, calls=%fused_computation.15 | custom fusion | flops 2048 | bytes 1118212 | tf_op jit(solution)/shard_map/scatter-add | solution.py:82
  167.1 5.5 %copy.385 = f32[8,16384]{1,0:T(8,128)S(1)} copy(f32[8,16384]{0,1:T(8,128)} %scatter_custom_fusion) | data formatting | bytes 1048576 | tf_op jit(solution)/shard_map/scatter-add | solution.py:82
  173.1 2.8 collective-permute-start.20
  175.9 1.3 collective-permute-start.19
  177.2 6.6 %collective-permute-start.18 = (f32[8,1]{1,0:T(8,128)S(1)}, f32[8,1]{1,0:T(8,128)S(1)}, u32[]{:S(2)}, u32[]{:S(2)}) collective-permute-start(f32[8,1]{1,0:T(8,128)S(1)} %get-tuple-element.15), channel_id=1, source_target_pairs={{0,2},{2,4},{4,6},{6,8},{8,10},{10,12},{12,14},{14,16},{16,18},{18... | collective-permute-start | bytes 104 | tf_op jit(solution)/shard_map/ppermute | solution.py:31
  183.8 0.7 collective-permute-done.18
  184.6 0.7 fusion.50
  185.2 2.8 collective-permute-start.23
  188.1 1.3 collective-permute-start.22
  189.4 6.6 %collective-permute-start.21 = (f32[8,1]{1,0:T(8,128)S(1)}, f32[8,1]{1,0:T(8,128)S(1)}, u32[]{:S(2)}, u32[]{:S(2)}) collective-permute-start(f32[8,1]{1,0:T(8,128)S(1)} %get-tuple-element.13), channel_id=1, source_target_pairs={{0,2},{2,4},{4,6},{6,8},{8,10},{10,12},{12,14},{14,16},{16,18},{18... | collective-permute-start | bytes 104 | tf_op jit(solution)/shard_map/ppermute | solution.py:31
  196.0 0.6 convolution_bitcast_fusion.3
  197.2 2.8 collective-permute-start.26
  200.0 1.3 collective-permute-start.25
  201.3 6.7 %collective-permute-start.24 = (f32[8,1]{1,0:T(8,128)S(1)}, f32[8,1]{1,0:T(8,128)S(1)}, u32[]{:S(2)}, u32[]{:S(2)}) collective-permute-start(f32[8,1]{1,0:T(8,128)S(1)} %get-tuple-element.11), channel_id=1, source_target_pairs={{0,2},{2,4},{4,6},{6,8},{8,10},{10,12},{12,14},{14,16},{16,18},{18... | collective-permute-start | bytes 104 | tf_op jit(solution)/shard_map/ppermute | solution.py:31
  208.0 0.7 collective-permute-done.24
  208.7 0.7 fusion.38
  209.4 2.8 collective-permute-start.29
  212.2 1.9 collective-permute-start.33
  214.2 1.3 collective-permute-start.28
  215.5 6.6 %collective-permute-start.27 = (f32[8,1]{1,0:T(8,128)S(1)}, f32[8,1]{1,0:T(8,128)S(1)}, u32[]{:S(2)}, u32[]{:S(2)}) collective-permute-start(f32[8,1]{1,0:T(8,128)S(1)} %get-tuple-element.9), channel_id=1, source_target_pairs={{0,2},{2,4},{4,6},{6,8},{8,10},{10,12},{12,14},{14,16},{16,18},{18... | collective-permute-start | bytes 104 | tf_op jit(solution)/shard_map/ppermute | solution.py:31
  222.2 0.6 convolution_bitcast_fusion.1
  223.3 3.3 collective-permute-start.32
  226.7 1.3 collective-permute-start.31
  227.9 6.6 %collective-permute-start.30 = (f32[8,1]{1,0:T(8,128)S(1)}, f32[8,1]{1,0:T(8,128)S(1)}, u32[]{:S(2)}, u32[]{:S(2)}) collective-permute-start(f32[8,1]{1,0:T(8,128)S(1)} %get-tuple-element.7), channel_id=1, source_target_pairs={{0,2},{2,4},{4,6},{6,8},{8,10},{10,12},{12,14},{14,16},{16,18},{18... | collective-permute-start | bytes 104 | tf_op jit(solution)/shard_map/ppermute | solution.py:31
  234.6 0.6 convolution_bitcast_fusion
  235.7 2.1 scatter_custom_fusion.1
  237.9 237.3 %reduce-scatter.2.cloned.1.call-done = f32[64,128]{1,0:T(8,128)} async-done(((f32[2048,128]{1,0:T(8,128)}), f32[64,128]{1,0:T(8,128)}) %reduce-scatter.2.cloned.1.call-update) | async-done | bytes 32784 | tf_op jit(solution)/shard_map/reduce_scatter | solution.py:88
  475.2 24.3 %all-gather = f32[1024,128]{1,0:T(8,128)S(1)} all-gather(f32[64,128]{1,0:T(8,128)} %reduce-scatter.2.cloned.1.call-done), channel_id=2, replica_groups=mesh['group'=8,'mesh'=32,'comp'=2] {'group','comp'}, dimensions={0}, use_global_device_ids=true | all-gather | bytes 557056 | tf_op jit(solution)/shard_map/all_gather | solution.py:14
  499.5 0.6 reduce_sum.19
  (67 shorter events, 5.0 us)
Async XLA Ops:
  6.5 15.5 %copy-start = (f32[128,128]{1,0:T(8,128)S(1)}, f32[128,128]{1,0:T(8,128)}, u32[]{:S(2)}) copy-start(f32[128,128]{1,0:T(8,128)} %param.10) | copy-start | bytes 196612
  6.5 115.8 %copy-start.1 = (f32[1,1,8,128,128]{4,3,2,1,0:T(8,128)S(1)}, f32[1,1,8,128,128]{4,3,2,1,0:T(8,128)}, u32[]{:S(2)}) copy-start(f32[1,1,8,128,128]{4,3,2,1,0:T(8,128)} %param.11) | copy-start | bytes 1572868
  6.5 87.3 %all-gather.3.cloned.1.call-start = ((), (), s32[]{:S(2)}) async-start(), calls=%async_computation.1 | async-start | bytes 1081344 | tf_op jit(solution)/shard_map/all_gather | solution.py:71
  7.3 467.9 %reduce-scatter.2.cloned.1.call-start = ((), (), s32[]{:S(2)}) async-start(), calls=%async_computation.2 | async-start | bytes 1081344 | tf_op jit(solution)/shard_map/reduce_scatter | solution.py:88
  7.3 88.5 %collective-permute-start.1 = (f32[8,1]{1,0:T(8,128)S(1)}, f32[8,1]{1,0:T(8,128)S(1)}, u32[]{:S(2)}, u32[]{:S(2)}) collective-permute-start(f32[8,1]{1,0:T(8,128)S(1)} %broadcast.157), channel_id=1, source_target_pairs={{2,0},{4,2},{6,4},{8,6},{10,8},{12,10},{14,12},{16,14},{18,16},{20... | collective-permute-start | bytes 104 | tf_op jit(solution)/shard_map/ppermute | solution.py:32
  8.6 87.2 %collective-permute-start = (f32[8,1]{1,0:T(8,128)S(1)}, f32[8,1]{1,0:T(8,128)S(1)}, u32[]{:S(2)}, u32[]{:S(2)}) collective-permute-start(f32[8,1]{1,0:T(8,128)S(1)} %broadcast.157), channel_id=1, source_target_pairs={{0,2},{2,4},{4,6},{6,8},{8,10},{10,12},{12,14},{14,16},{16,18},{18... | collective-permute-start | bytes 104 | tf_op jit(solution)/shard_map/ppermute | solution.py:31
  13.2 132.6 %copy-start.3 = (s32[1,128]{1,0:T(1,128)S(1)}, s32[1,128]{1,0:T(1,128)}, u32[]{:S(2)}) copy-start(s32[1,128]{1,0:T(1,128)} %param.12) | copy-start | bytes 1540
  13.3 132.6 %copy-start.2 = (f32[1,1,8,128]{3,2,1,0:T(8,128)S(1)}, f32[1,1,8,128]{3,2,1,0:T(8,128)}, u32[]{:S(2)}) copy-start(f32[1,1,8,128]{3,2,1,0:T(8,128)} %param.13) | copy-start | bytes 12292
  13.3 82.6 %collective-permute-start.2 = (f32[8,16384]{1,0:T(8,128)S(1)}, f32[8,16384]{1,0:T(8,128)S(1)}, u32[]{:S(2)}, u32[]{:S(2)}) collective-permute-start(f32[8,16384]{1,0:T(8,128)S(1)} %broadcast.154.clone), channel_id=1, source_target_pairs={{0,1},{1,0},{2,3},{3,2},{4,5},{5,4},{6,7},{7,6},{8,9},{9,8},{10,11... | collective-permute-start | bytes 1572872 | tf_op jit(solution)/shard_map/ppermute | solution.py:21
  97.5 13.1 %collective-permute-start.5 = (f32[8,16384]{1,0:T(8,128)S(1)}, f32[8,16384]{1,0:T(8,128)S(1)}, u32[]{:S(2)}, u32[]{:S(2)}) collective-permute-start(f32[8,16384]{1,0:T(8,128)S(1)} %fusion.8), channel_id=1, source_target_pairs={{0,1},{1,0},{2,3},{3,2},{4,5},{5,4},{6,7},{7,6},{8,9},{9,8},{10,11... | collective-permute-start | bytes 1572872 | tf_op jit(solution)/shard_map/ppermute | solution.py:21
  104.6 5.3 %collective-permute-start.4 = (f32[8,1]{1,0:T(8,128)S(1)}, f32[8,1]{1,0:T(8,128)S(1)}, u32[]{:S(2)}, u32[]{:S(2)}) collective-permute-start(f32[8,1]{1,0:T(8,128)S(1)} %get-tuple-element.26), channel_id=1, source_target_pairs={{2,0},{4,2},{6,4},{8,6},{10,8},{12,10},{14,12},{16,14},{18,16},{20... | collective-permute-start | bytes 104 | tf_op jit(solution)/shard_map/ppermute | solution.py:32
  105.9 4.7 collective-permute-start.3
  112.6 9.7 %collective-permute-start.8 = (f32[8,16384]{1,0:T(8,128)S(1)}, f32[8,16384]{1,0:T(8,128)S(1)}, u32[]{:S(2)}, u32[]{:S(2)}) collective-permute-start(f32[8,16384]{1,0:T(8,128)S(1)} %fusion.10), channel_id=1, source_target_pairs={{0,1},{1,0},{2,3},{3,2},{4,5},{5,4},{6,7},{7,6},{8,9},{9,8},{10,11... | collective-permute-start | bytes 1572872 | tf_op jit(solution)/shard_map/ppermute | solution.py:21
  115.7 6.4 %collective-permute-start.7 = (f32[8,1]{1,0:T(8,128)S(1)}, f32[8,1]{1,0:T(8,128)S(1)}, u32[]{:S(2)}, u32[]{:S(2)}) collective-permute-start(f32[8,1]{1,0:T(8,128)S(1)} %get-tuple-element.24), channel_id=1, source_target_pairs={{2,0},{4,2},{6,4},{8,6},{10,8},{12,10},{14,12},{16,14},{18,16},{20... | collective-permute-start | bytes 104 | tf_op jit(solution)/shard_map/ppermute | solution.py:32
  117.0 5.3 %collective-permute-start.6 = (f32[8,1]{1,0:T(8,128)S(1)}, f32[8,1]{1,0:T(8,128)S(1)}, u32[]{:S(2)}, u32[]{:S(2)}) collective-permute-start(f32[8,1]{1,0:T(8,128)S(1)} %get-tuple-element.23), channel_id=1, source_target_pairs={{0,2},{2,4},{4,6},{6,8},{8,10},{10,12},{12,14},{14,16},{16,18},{18... | collective-permute-start | bytes 104 | tf_op jit(solution)/shard_map/ppermute | solution.py:31
  122.8 9.4 %collective-permute-start.11 = (f32[8,16384]{1,0:T(8,128)S(1)}, f32[8,16384]{1,0:T(8,128)S(1)}, u32[]{:S(2)}, u32[]{:S(2)}) collective-permute-start(f32[8,16384]{1,0:T(8,128)S(1)} %fusion.12), channel_id=1, source_target_pairs={{0,1},{1,0},{2,3},{3,2},{4,5},{5,4},{6,7},{7,6},{8,9},{9,8},{10,11... | collective-permute-start | bytes 1572872 | tf_op jit(solution)/shard_map/ppermute | solution.py:21
  125.7 5.8 %collective-permute-start.10 = (f32[8,1]{1,0:T(8,128)S(1)}, f32[8,1]{1,0:T(8,128)S(1)}, u32[]{:S(2)}, u32[]{:S(2)}) collective-permute-start(f32[8,1]{1,0:T(8,128)S(1)} %get-tuple-element.22), channel_id=1, source_target_pairs={{2,0},{4,2},{6,4},{8,6},{10,8},{12,10},{14,12},{16,14},{18,16},{20... | collective-permute-start | bytes 104 | tf_op jit(solution)/shard_map/ppermute | solution.py:32
  126.9 5.3 %collective-permute-start.9 = (f32[8,1]{1,0:T(8,128)S(1)}, f32[8,1]{1,0:T(8,128)S(1)}, u32[]{:S(2)}, u32[]{:S(2)}) collective-permute-start(f32[8,1]{1,0:T(8,128)S(1)} %get-tuple-element.21), channel_id=1, source_target_pairs={{0,2},{2,4},{4,6},{6,8},{8,10},{10,12},{12,14},{14,16},{16,18},{18... | collective-permute-start | bytes 104 | tf_op jit(solution)/shard_map/ppermute | solution.py:31
  133.1 9.4 %collective-permute-start.14 = (f32[8,16384]{1,0:T(8,128)S(1)}, f32[8,16384]{1,0:T(8,128)S(1)}, u32[]{:S(2)}, u32[]{:S(2)}) collective-permute-start(f32[8,16384]{1,0:T(8,128)S(1)} %fusion.14), channel_id=1, source_target_pairs={{0,1},{1,0},{2,3},{3,2},{4,5},{5,4},{6,7},{7,6},{8,9},{9,8},{10,11... | collective-permute-start | bytes 1572872 | tf_op jit(solution)/shard_map/ppermute | solution.py:21
  136.0 6.4 %collective-permute-start.13 = (f32[8,1]{1,0:T(8,128)S(1)}, f32[8,1]{1,0:T(8,128)S(1)}, u32[]{:S(2)}, u32[]{:S(2)}) collective-permute-start(f32[8,1]{1,0:T(8,128)S(1)} %get-tuple-element.20), channel_id=1, source_target_pairs={{2,0},{4,2},{6,4},{8,6},{10,8},{12,10},{14,12},{16,14},{18,16},{20... | collective-permute-start | bytes 104 | tf_op jit(solution)/shard_map/ppermute | solution.py:32
  137.3 5.3 %collective-permute-start.12 = (f32[8,1]{1,0:T(8,128)S(1)}, f32[8,1]{1,0:T(8,128)S(1)}, u32[]{:S(2)}, u32[]{:S(2)}) collective-permute-start(f32[8,1]{1,0:T(8,128)S(1)} %get-tuple-element.19), channel_id=1, source_target_pairs={{0,2},{2,4},{4,6},{6,8},{8,10},{10,12},{12,14},{14,16},{16,18},{18... | collective-permute-start | bytes 104 | tf_op jit(solution)/shard_map/ppermute | solution.py:31
  143.1 10.8 %collective-permute-start.17 = (f32[8,16384]{1,0:T(8,128)S(1)}, f32[8,16384]{1,0:T(8,128)}, u32[]{:S(2)}, u32[]{:S(2)}) collective-permute-start(f32[8,16384]{1,0:T(8,128)S(1)} %fusion.16), channel_id=1, source_target_pairs={{0,1},{1,0},{2,3},{3,2},{4,5},{5,4},{6,7},{7,6},{8,9},{9,8},{10,11... | collective-permute-start | bytes 1572872 | tf_op jit(solution)/shard_map/ppermute | solution.py:21
  146.6 6.5 %collective-permute-start.16 = (f32[8,1]{1,0:T(8,128)S(1)}, f32[8,1]{1,0:T(8,128)S(1)}, u32[]{:S(2)}, u32[]{:S(2)}) collective-permute-start(f32[8,1]{1,0:T(8,128)S(1)} %get-tuple-element.18), channel_id=1, source_target_pairs={{2,0},{4,2},{6,4},{8,6},{10,8},{12,10},{14,12},{16,14},{18,16},{20... | collective-permute-start | bytes 104 | tf_op jit(solution)/shard_map/ppermute | solution.py:32
  147.9 5.9 %collective-permute-start.15 = (f32[8,1]{1,0:T(8,128)S(1)}, f32[8,1]{1,0:T(8,128)S(1)}, u32[]{:S(2)}, u32[]{:S(2)}) collective-permute-start(f32[8,1]{1,0:T(8,128)S(1)} %get-tuple-element.17), channel_id=1, source_target_pairs={{0,2},{2,4},{4,6},{6,8},{8,10},{10,12},{12,14},{14,16},{16,18},{18... | collective-permute-start | bytes 104 | tf_op jit(solution)/shard_map/ppermute | solution.py:31
  173.1 11.5 %collective-permute-start.20 = (f32[8,16384]{1,0:T(8,128)S(1)}, f32[8,16384]{1,0:T(8,128)S(1)}, u32[]{:S(2)}, u32[]{:S(2)}) collective-permute-start(f32[8,16384]{1,0:T(8,128)S(1)} %fusion.5), channel_id=1, source_target_pairs={{0,1},{1,0},{2,3},{3,2},{4,5},{5,4},{6,7},{7,6},{8,9},{9,8},{10,11... | collective-permute-start | bytes 1572872 | tf_op jit(solution)/shard_map/ppermute | solution.py:21
  175.9 7.9 %collective-permute-start.19 = (f32[8,1]{1,0:T(8,128)S(1)}, f32[8,1]{1,0:T(8,128)S(1)}, u32[]{:S(2)}, u32[]{:S(2)}) collective-permute-start(f32[8,1]{1,0:T(8,128)S(1)} %get-tuple-element.16), channel_id=1, source_target_pairs={{2,0},{4,2},{6,4},{8,6},{10,8},{12,10},{14,12},{16,14},{18,16},{20... | collective-permute-start | bytes 104 | tf_op jit(solution)/shard_map/ppermute | solution.py:32
  177.2 7.4 %collective-permute-start.18 = (f32[8,1]{1,0:T(8,128)S(1)}, f32[8,1]{1,0:T(8,128)S(1)}, u32[]{:S(2)}, u32[]{:S(2)}) collective-permute-start(f32[8,1]{1,0:T(8,128)S(1)} %get-tuple-element.15), channel_id=1, source_target_pairs={{0,2},{2,4},{4,6},{6,8},{8,10},{10,12},{12,14},{14,16},{16,18},{18... | collective-permute-start | bytes 104 | tf_op jit(solution)/shard_map/ppermute | solution.py:31
  185.2 11.5 %collective-permute-start.23 = (f32[8,16384]{1,0:T(8,128)S(1)}, f32[8,16384]{1,0:T(8,128)S(1)}, u32[]{:S(2)}, u32[]{:S(2)}) collective-permute-start(f32[8,16384]{1,0:T(8,128)S(1)} %fusion.50), channel_id=1, source_target_pairs={{0,1},{1,0},{2,3},{3,2},{4,5},{5,4},{6,7},{7,6},{8,9},{9,8},{10,11... | collective-permute-start | bytes 1572872 | tf_op jit(solution)/shard_map/ppermute | solution.py:21
  188.1 8.5 %collective-permute-start.22 = (f32[8,1]{1,0:T(8,128)S(1)}, f32[8,1]{1,0:T(8,128)S(1)}, u32[]{:S(2)}, u32[]{:S(2)}) collective-permute-start(f32[8,1]{1,0:T(8,128)S(1)} %get-tuple-element.14), channel_id=1, source_target_pairs={{2,0},{4,2},{6,4},{8,6},{10,8},{12,10},{14,12},{16,14},{18,16},{20... | collective-permute-start | bytes 104 | tf_op jit(solution)/shard_map/ppermute | solution.py:32
  189.4 7.4 %collective-permute-start.21 = (f32[8,1]{1,0:T(8,128)S(1)}, f32[8,1]{1,0:T(8,128)S(1)}, u32[]{:S(2)}, u32[]{:S(2)}) collective-permute-start(f32[8,1]{1,0:T(8,128)S(1)} %get-tuple-element.13), channel_id=1, source_target_pairs={{0,2},{2,4},{4,6},{6,8},{8,10},{10,12},{12,14},{14,16},{16,18},{18... | collective-permute-start | bytes 104 | tf_op jit(solution)/shard_map/ppermute | solution.py:31
  197.2 11.6 %collective-permute-start.26 = (f32[8,16384]{1,0:T(8,128)S(1)}, f32[8,16384]{1,0:T(8,128)S(1)}, u32[]{:S(2)}, u32[]{:S(2)}) collective-permute-start(f32[8,16384]{1,0:T(8,128)S(1)} %fusion.44), channel_id=1, source_target_pairs={{0,1},{1,0},{2,3},{3,2},{4,5},{5,4},{6,7},{7,6},{8,9},{9,8},{10,11... | collective-permute-start | bytes 1572872 | tf_op jit(solution)/shard_map/ppermute | solution.py:21
  200.0 8.0 %collective-permute-start.25 = (f32[8,1]{1,0:T(8,128)S(1)}, f32[8,1]{1,0:T(8,128)S(1)}, u32[]{:S(2)}, u32[]{:S(2)}) collective-permute-start(f32[8,1]{1,0:T(8,128)S(1)} %get-tuple-element.12), channel_id=1, source_target_pairs={{2,0},{4,2},{6,4},{8,6},{10,8},{12,10},{14,12},{16,14},{18,16},{20... | collective-permute-start | bytes 104 | tf_op jit(solution)/shard_map/ppermute | solution.py:32
  201.3 7.4 %collective-permute-start.24 = (f32[8,1]{1,0:T(8,128)S(1)}, f32[8,1]{1,0:T(8,128)S(1)}, u32[]{:S(2)}, u32[]{:S(2)}) collective-permute-start(f32[8,1]{1,0:T(8,128)S(1)} %get-tuple-element.11), channel_id=1, source_target_pairs={{0,2},{2,4},{4,6},{6,8},{8,10},{10,12},{12,14},{14,16},{16,18},{18... | collective-permute-start | bytes 104 | tf_op jit(solution)/shard_map/ppermute | solution.py:31
  209.4 13.5 %collective-permute-start.29 = (f32[8,16384]{1,0:T(8,128)S(1)}, f32[8,16384]{1,0:T(8,128)S(1)}, u32[]{:S(2)}, u32[]{:S(2)}) collective-permute-start(f32[8,16384]{1,0:T(8,128)S(1)} %fusion.38), channel_id=1, source_target_pairs={{0,1},{1,0},{2,3},{3,2},{4,5},{5,4},{6,7},{7,6},{8,9},{9,8},{10,11... | collective-permute-start | bytes 1572872 | tf_op jit(solution)/shard_map/ppermute | solution.py:21
  212.2 22.9 %collective-permute-start.33 = (f32[8,16384]{1,0:T(8,128)S(1)}, f32[8,16384]{1,0:T(8,128)S(1)}, u32[]{:S(2)}, u32[]{:S(2)}) collective-permute-start(f32[8,16384]{1,0:T(8,128)S(1)} %fusion.18), channel_id=1, source_target_pairs={{0,1},{1,0},{2,3},{3,2},{4,5},{5,4},{6,7},{7,6},{8,9},{9,8},{10,11... | collective-permute-start | bytes 1572872 | tf_op jit(solution)/shard_map/ppermute | solution.py:21
  214.2 8.5 %collective-permute-start.28 = (f32[8,1]{1,0:T(8,128)S(1)}, f32[8,1]{1,0:T(8,128)S(1)}, u32[]{:S(2)}, u32[]{:S(2)}) collective-permute-start(f32[8,1]{1,0:T(8,128)S(1)} %get-tuple-element.10), channel_id=1, source_target_pairs={{2,0},{4,2},{6,4},{8,6},{10,8},{12,10},{14,12},{16,14},{18,16},{20... | collective-permute-start | bytes 104 | tf_op jit(solution)/shard_map/ppermute | solution.py:32
  215.5 7.4 %collective-permute-start.27 = (f32[8,1]{1,0:T(8,128)S(1)}, f32[8,1]{1,0:T(8,128)S(1)}, u32[]{:S(2)}, u32[]{:S(2)}) collective-permute-start(f32[8,1]{1,0:T(8,128)S(1)} %get-tuple-element.9), channel_id=1, source_target_pairs={{0,2},{2,4},{4,6},{6,8},{8,10},{10,12},{12,14},{14,16},{16,18},{18... | collective-permute-start | bytes 104 | tf_op jit(solution)/shard_map/ppermute | solution.py:31
  223.3 12.0 %collective-permute-start.32 = (f32[8,16384]{1,0:T(8,128)S(1)}, f32[8,16384]{1,0:T(8,128)S(1)}, u32[]{:S(2)}, u32[]{:S(2)}) collective-permute-start(f32[8,16384]{1,0:T(8,128)S(1)} %fusion.32), channel_id=1, source_target_pairs={{0,1},{1,0},{2,3},{3,2},{4,5},{5,4},{6,7},{7,6},{8,9},{9,8},{10,11... | collective-permute-start | bytes 1572872 | tf_op jit(solution)/shard_map/ppermute | solution.py:21
  226.7 8.5 %collective-permute-start.31 = (f32[8,1]{1,0:T(8,128)S(1)}, f32[8,1]{1,0:T(8,128)S(1)}, u32[]{:S(2)}, u32[]{:S(2)}) collective-permute-start(f32[8,1]{1,0:T(8,128)S(1)} %get-tuple-element.8), channel_id=1, source_target_pairs={{2,0},{4,2},{6,4},{8,6},{10,8},{12,10},{14,12},{16,14},{18,16},{20... | collective-permute-start | bytes 104 | tf_op jit(solution)/shard_map/ppermute | solution.py:32
  227.9 7.4 %collective-permute-start.30 = (f32[8,1]{1,0:T(8,128)S(1)}, f32[8,1]{1,0:T(8,128)S(1)}, u32[]{:S(2)}, u32[]{:S(2)}) collective-permute-start(f32[8,1]{1,0:T(8,128)S(1)} %get-tuple-element.7), channel_id=1, source_target_pairs={{0,2},{2,4},{4,6},{6,8},{8,10},{10,12},{12,14},{14,16},{16,18},{18... | collective-permute-start | bytes 104 | tf_op jit(solution)/shard_map/ppermute | solution.py:31
Sparse Core Ops, SparseCore 0:
  10.5 83.2 all-gather.2
  238.0 237.1 reduce-scatter.1
